TPU v7x, 32 devices: a whole 2x2x4 slice. The times are simulated.
32 devices in a mesh: sub: 8 (over z, y), col: 4 (over x, core).
Axes of the slice: x: 2, y: 2, z: 4, core: 2. Of those that a mesh axis runs over, the one named last changes fastest.
Arguments:
- rhs: bfloat16 [32, 1024, 128], P(('sub', 'col')), may hold values from -64 to 64
- schur: bfloat16 [32, 1024, 1024], P(('sub', 'col')), may hold values from -1 to 3
- local_inverse: bfloat16 [32, 1024, 1024], P(('sub', 'col')), may hold values from -1 to 2
- basis: bfloat16 [32, 8, 1024], P(('sub', 'col')), may hold values from -0.75 to 0.75
- coarse_inverse: bfloat16 [256, 256], P('sub', 'col'), may hold values from -1 to 2
- primal_index: int32 [32, 8], P(('sub', 'col')), may hold values from 0 to 255, as said below
- neighbour_dof: int32 [32, 1024], P(('sub', 'col')), may hold values from 0 to 1023, as said below
Outputs:
- solution: bfloat16 [32, 1024, 128], P(('sub', 'col'))
Inputs may be any that keep to these rules, and one draw needn't show every extreme that they name: `neighbour_dof`: each subdomain's unknowns in one shared block name places in the neighbour's facing block (for [0, 256) the neighbour's [256, 512), and so on), and the neighbour's entry names the place back. `primal_index`: every coarse unknown is named exactly once over all subdomains.
All inputs are finite; a program needn't handle non-finite values.
Results may differ from a plain program's by a relative error of at most 0.004.
The roundings to bfloat16 on the way count: a program that leaves them out, or rounds other values in their place, can miss the bound.
Values may be sent and summed in bfloat16 or wider, within the bound.
A program may use at most 64 MiB of HBM per device.

v0:
```python
import jax
import jax.numpy as jnp
from jax import lax
from jax.sharding import PartitionSpec as P


def from_behind(value, axis, steps):
    count = lax.axis_size(axis)
    pairs = [(source, (source + steps) % count) for source in range(count)]
    return lax.ppermute(value, axis, pairs)


def on_device(rhs, schur, local_inverse, basis, coarse_inverse, primal_index, neighbour_dof):
    link_table = neighbour_dof[0]
    face_size = link_table.shape[0] // 4
    cases = rhs.shape[2]
    offsets = (face_size, 0, 3 * face_size, 2 * face_size)
    places = []
    for number in range(4):
        places.append(link_table[number * face_size : (number + 1) * face_size] - offsets[number])
    schur_own = schur[0]
    inverse_own = local_inverse[0]
    basis_own = basis[0]
    index_own = primal_index[0]
    column_width = coarse_inverse.shape[1]
    column_base = lax.axis_index("col") * column_width

    def combine(field, incoming):
        collected = [
            jnp.take(incoming[number].astype(jnp.float32), places[number], axis=0)
            for number in range(4)
        ]
        return field + jnp.concatenate(collected, axis=0)

    def assemble(field):
        from_below = from_behind(field[face_size : 2 * face_size], "sub", 1)
        from_above = from_behind(field[:face_size], "sub", -1)
        from_left = from_behind(field[3 * face_size :].astype(jnp.bfloat16), "col", 1).astype(
            jnp.float32
        )
        from_right = from_behind(field[2 * face_size : 3 * face_size], "col", -1)
        return combine(field, (from_below, from_above, from_left, from_right))

    def inner(left_field, right_field):
        return lax.psum(0.5 * jnp.sum(left_field * right_field, axis=0), ("sub", "col"))

    residual = assemble(rhs[0].astype(jnp.float32))
    weighted = (residual * 0.5).astype(jnp.bfloat16)
    local_part = jnp.dot(inverse_own, weighted, preferred_element_type=jnp.float32)
    coarse_load = jnp.dot(basis_own, weighted, preferred_element_type=jnp.float32).astype(
        jnp.bfloat16
    )
    start_block = jnp.zeros((column_width, cases), jnp.bfloat16)
    values = lax.all_gather(coarse_load, ("sub", "col"), axis=0, tiled=True)
    indices = lax.all_gather(index_own, ("sub", "col"), axis=0, tiled=True)
    spots = indices - column_base
    spots = jnp.where((spots >= 0) & (spots < column_width), spots, column_width)
    column_part = start_block.at[spots].set(values, mode="drop")
    partial_rows = jnp.dot(coarse_inverse, column_part, preferred_element_type=jnp.float32)
    start_taken = jnp.zeros((index_own.shape[0], cases), jnp.bfloat16)
    block_rows = lax.psum(partial_rows, "col").astype(jnp.bfloat16)
    piece = lax.all_gather(block_rows, "sub", axis=0, tiled=True)
    spots = index_own
    count = piece.shape[0]
    valid = (spots >= 0) & (spots < count)
    rows = jnp.take(piece, jnp.clip(spots, 0, count - 1), axis=0)
    taken = jnp.where(valid[:, None], rows, start_taken)
    correction = lax.dot_general(
        basis_own, taken, (((0,), (0,)), ((), ())), preferred_element_type=jnp.float32
    )
    first = assemble((local_part + correction) * 0.5)
    rz_first = inner(residual, first)
    image = assemble(
        jnp.dot(schur_own, first.astype(jnp.bfloat16), preferred_element_type=jnp.float32)
    )
    alpha = rz_first / inner(first, image)
    return (alpha * first).astype(jnp.bfloat16)[None]


def solution(mesh):
    return jax.shard_map(
        on_device,
        mesh=mesh,
        in_specs=(
            P(("sub", "col"), None, None),
            P(("sub", "col"), None, None),
            P(("sub", "col"), None, None),
            P(("sub", "col"), None, None),
            P("sub", "col"),
            P(("sub", "col"), None),
            P(("sub", "col"), None),
        ),
        out_specs=P(("sub", "col"), None, None),
        check_vma=False,
    )
```

profile of v0, /device:TPU:0, one launch (start us, length us, event | category | flops | bytes accessed | tf_op | source)
XLA Modules:
  0.0 225.9 jit_solution(8289083633915082191)
XLA Ops:
  0.0 1.2 copy.8
  1.3 3.1 %collective-permute-start = (f32[256,128]{0,1:T(8,128)S(1)}, f32[256,128]{0,1:T(8,128)S(1)}, u32[]{:S(2)}, u32[]{:S(2)}) collective-permute-start(f32[256,128]{0,1:T(8,128)S(1)} %get-tuple-element.16), channel_id=1, source_target_pairs={{0,4},{4,8},{8,12},{12,16},{16,20},{20,24},{24,28},{28,0},{1,5},{5... | collective-permute-start | bytes 393224 | tf_op jit(solution)/shard_map/ppermute | solution.py:10
  4.4 3.1 %collective-permute-start.1 = (f32[256,128]{0,1:T(8,128)S(1)}, f32[256,128]{0,1:T(8,128)S(1)}, u32[]{:S(2)}, u32[]{:S(2)}) collective-permute-start(f32[256,128]{0,1:T(8,128)S(1)} %get-tuple-element.17), channel_id=1, source_target_pairs={{0,28},{4,0},{8,4},{12,8},{16,12},{20,16},{24,20},{28,24},{1,29},{... | collective-permute-start | bytes 393224 | tf_op jit(solution)/shard_map/ppermute | solution.py:10
  12.6 37.7 %all-reduce = s32[256]{0:T(256)S(1)} all-reduce(s32[256]{0:T(256)S(1)} %bitcast_dynamic-update-slice_fusion), channel_id=2, replica_groups=mesh['sub'=8,'col'=4] {'sub','col'}, use_global_device_ids=true, to_apply=%add | all-reduce | flops 256 | bytes 2048
  52.9 1.2 broadcast_select_fusion.9
  57.4 41.2 %all_gather.10 = bf16[256,128]{1,0:T(8,128)(2,1)S(1)} all-gather(bf16[8,128]{1,0:T(8,128)(2,1)S(1)} %fusion.9), channel_id=1, replica_groups=mesh['sub'=8,'col'=4] {'sub','col'}, dimensions={0}, use_global_device_ids=true | all-gather | bytes 67584 | tf_op jit(solution)/shard_map/all_gather | solution.py:54
  98.6 1.3 scatter_custom_fusion
  100.0 10.3 %psum.21 = bf16[32,128]{1,0:T(8,128)(2,1)S(1)} all-reduce(f32[32,128]{1,0:T(8,128)S(1)} %convolution_bitcast_fusion), channel_id=1, replica_groups=mesh['sub'=8,'col'=4] {'col'}, use_global_device_ids=true, to_apply=%region_1.3 | all-reduce | flops 4096 | bytes 24576 | tf_op jit(solution)/shard_map/psum | solution.py:61
  110.4 30.5 %all_gather.11 = bf16[256,128]{1,0:T(8,128)(2,1)S(1)} all-gather(bf16[32,128]{1,0:T(8,128)(2,1)S(1)} %psum.21), channel_id=1, replica_groups=mesh['sub'=8,'col'=4] {'sub'}, dimensions={0}, use_global_device_ids=true | all-gather | bytes 73728 | tf_op jit(solution)/shard_map/all_gather | solution.py:62
  140.9 1.6 fusion.2
  143.2 1.4 fusion.8
  146.7 4.7 %collective-permute-start.5 = (f32[256,128]{0,1:T(8,128)}, f32[256,128]{0,1:T(8,128)S(1)}, u32[]{:S(2)}, u32[]{:S(2)}) collective-permute-start(f32[256,128]{0,1:T(8,128)} %get-tuple-element.15), channel_id=1, source_target_pairs={{0,28},{4,0},{8,4},{12,8},{16,12},{20,16},{24,20},{28,24},{1,29},{... | collective-permute-start | bytes 393224 | tf_op jit(solution)/shard_map/ppermute | solution.py:10
  151.9 1.3 broadcast_select_fusion.8
  153.3 2.2 collective-permute-done.6
  163.4 2.0 collective-permute-start.9
  165.5 1.4 collective-permute-start.11
  167.8 1.3 gather_fusion.11
  170.2 1.2 broadcast_select_fusion.1
  172.4 1.4 gather_fusion.10
  174.8 1.3 broadcast_select_fusion.2
  177.1 1.3 gather_fusion.9
  181.1 1.3 gather_fusion.12
  183.5 1.5 fusion.15
  185.0 39.9 %all-reduce.1 = (f32[128]{0:T(128)S(1)}, f32[128]{0:T(128)S(1)}) all-reduce(f32[128]{0:T(128)S(1)} %broadcast_multiply_fusion.1, f32[128]{0:T(128)S(1)} %broadcast_multiply_fusion), channel_id=1, replica_groups=mesh['sub'=8,'col'=4] {'sub','col'}, use_global_device_ids=true, to_apply=%region_3.5 | all-reduce | flops 256 | bytes 2048 | tf_op jit(solution)/shard_map/psum | solution.py:45
  (124 shorter events, 31.6 us)
Async XLA Ops:
  0.0 140.9 %copy-start = (bf16[1,1024,1024]{2,1,0:T(8,128)(2,1)S(1)}, bf16[1,1024,1024]{2,1,0:T(8,128)(2,1)}, u32[]{:S(2)}) copy-start(bf16[1,1024,1024]{2,1,0:T(8,128)(2,1)} %param.11) | copy-start | bytes 6291460
  0.0 9.0 %copy-start.9 = (s32[1,1024]{1,0:T(1,128)S(1)}, s32[1,1024]{1,0:T(1,128)}, u32[]{:S(2)}) copy-start(s32[1,1024]{1,0:T(1,128)} %param.15) | copy-start | bytes 12292
  0.0 11.2 %copy-start.12 = (s32[1,8]{1,0:T(1,128)S(1)}, s32[1,8]{1,0:T(1,128)}, u32[]{:S(2)}) copy-start(s32[1,8]{1,0:T(1,128)} %param.14) | copy-start | bytes 100
  1.3 52.8 %collective-permute-start = (f32[256,128]{0,1:T(8,128)S(1)}, f32[256,128]{0,1:T(8,128)S(1)}, u32[]{:S(2)}, u32[]{:S(2)}) collective-permute-start(f32[256,128]{0,1:T(8,128)S(1)} %get-tuple-element.16), channel_id=1, source_target_pairs={{0,4},{4,8},{8,12},{12,16},{16,20},{20,24},{24,28},{28,0},{1,5},{5... | collective-permute-start | bytes 393224 | tf_op jit(solution)/shard_map/ppermute | solution.py:10
  4.4 50.7 %collective-permute-start.1 = (f32[256,128]{0,1:T(8,128)S(1)}, f32[256,128]{0,1:T(8,128)S(1)}, u32[]{:S(2)}, u32[]{:S(2)}) collective-permute-start(f32[256,128]{0,1:T(8,128)S(1)} %get-tuple-element.17), channel_id=1, source_target_pairs={{0,28},{4,0},{8,4},{12,8},{16,12},{20,16},{24,20},{28,24},{1,29},{... | collective-permute-start | bytes 393224 | tf_op jit(solution)/shard_map/ppermute | solution.py:10
  7.5 48.6 %collective-permute-start.3 = (f32[256,128]{0,1:T(8,128)S(1)}, f32[256,128]{0,1:T(8,128)S(1)}, u32[]{:S(2)}, u32[]{:S(2)}) collective-permute-start(f32[256,128]{0,1:T(8,128)S(1)} %get-tuple-element.18), channel_id=1, source_target_pairs={{0,3},{1,0},{2,1},{3,2},{4,7},{5,4},{6,5},{7,6},{8,11},{9,8},{10,9... | collective-permute-start | bytes 393224 | tf_op jit(solution)/shard_map/ppermute | solution.py:10
  9.0 42.5 %collective-permute-start.2 = (bf16[256,128]{1,0:T(8,128)(2,1)S(1)}, bf16[256,128]{1,0:T(8,128)(2,1)S(1)}, u32[]{:S(2)}, u32[]{:S(2)}) collective-permute-start(bf16[256,128]{1,0:T(8,128)(2,1)S(1)} %slice_bitcast_fusion.3), channel_id=1, source_target_pairs={{0,1},{1,2},{2,3},{3,0},{4,5},{5,6},{6,7},{7,4},{8,9},{9,10},{10,1... | collective-permute-start | bytes 196616 | tf_op jit(solution)/shard_map/ppermute | solution.py:10
  55.0 2.0 copy-start.6
  55.0 2.1 copy-start.8
  55.0 2.1 copy-start.4
  56.0 43.9 %copy-start.3 = (bf16[32,64]{1,0:T(8,128)(2,1)S(1)}, bf16[32,64]{1,0:T(8,128)(2,1)}, u32[]{:S(2)}) copy-start(bf16[32,64]{1,0:T(8,128)(2,1)} %param.13) | copy-start | bytes 12292
  57.1 86.1 %copy-start.10 = (pred[8]{0:T(512)(128)(4,1)S(1)}, pred[8]{0:T(512)(128)(4,1)}, u32[]{:S(2)}) copy-start(pred[8]{0:T(512)(128)(4,1)} %and_bitcast_fusion) | copy-start | bytes 28
  57.1 86.1 %copy-start.11 = (pred[8]{0:T(512)(128)(4,1)S(1)}, pred[8]{0:T(512)(128)(4,1)}, u32[]{:S(2)}) copy-start(pred[8]{0:T(512)(128)(4,1)} %compare_and_fusion.4) | copy-start | bytes 28
  146.7 9.7 %collective-permute-start.4 = (f32[256,128]{0,1:T(8,128)}, f32[256,128]{0,1:T(8,128)S(1)}, u32[]{:S(2)}, u32[]{:S(2)}) collective-permute-start(f32[256,128]{0,1:T(8,128)} %get-tuple-element.13), channel_id=1, source_target_pairs={{0,4},{4,8},{8,12},{12,16},{16,20},{20,24},{24,28},{28,0},{1,5},{5... | collective-permute-start | bytes 393224 | tf_op jit(solution)/shard_map/ppermute | solution.py:10
  146.7 10.6 %collective-permute-start.5 = (f32[256,128]{0,1:T(8,128)}, f32[256,128]{0,1:T(8,128)S(1)}, u32[]{:S(2)}, u32[]{:S(2)}) collective-permute-start(f32[256,128]{0,1:T(8,128)} %get-tuple-element.15), channel_id=1, source_target_pairs={{0,28},{4,0},{8,4},{12,8},{16,12},{20,16},{24,20},{28,24},{1,29},{... | collective-permute-start | bytes 393224 | tf_op jit(solution)/shard_map/ppermute | solution.py:10
  151.4 6.8 %collective-permute-start.7 = (f32[256,128]{0,1:T(8,128)}, f32[256,128]{0,1:T(8,128)}, u32[]{:S(2)}, u32[]{:S(2)}) collective-permute-start(f32[256,128]{0,1:T(8,128)} %get-tuple-element.14), channel_id=1, source_target_pairs={{0,3},{1,0},{2,1},{3,2},{4,7},{5,4},{6,5},{7,6},{8,11},{9,8},{10,9... | collective-permute-start | bytes 393224 | tf_op jit(solution)/shard_map/ppermute | solution.py:10
  151.4 4.0 %collective-permute-start.6 = (bf16[256,128]{0,1:T(8,128)(2,1)S(1)}, bf16[256,128]{0,1:T(8,128)(2,1)S(1)}, u32[]{:S(2)}, u32[]{:S(2)}) collective-permute-start(bf16[256,128]{0,1:T(8,128)(2,1)S(1)} %slice.134), channel_id=1, source_target_pairs={{0,1},{1,2},{2,3},{3,0},{4,5},{5,6},{6,7},{7,4},{8,9},{9,10},{10,1... | collective-permute-start | bytes 196616 | tf_op jit(solution)/shard_map/ppermute | solution.py:10
  160.1 1.6 copy-start.1
  162.6 4.3 %collective-permute-start.10 = (bf16[256,128]{0,1:T(8,128)(2,1)S(1)}, bf16[256,128]{0,1:T(8,128)(2,1)}, u32[]{:S(2)}, u32[]{:S(2)}) collective-permute-start(bf16[256,128]{0,1:T(8,128)(2,1)S(1)} %slice.133), channel_id=1, source_target_pairs={{0,1},{1,2},{2,3},{3,0},{4,5},{5,6},{6,7},{7,4},{8,9},{9,10},{10,1... | collective-permute-start | bytes 196616 | tf_op jit(solution)/shard_map/ppermute | solution.py:10
  163.4 8.0 %collective-permute-start.9 = (f32[256,128]{0,1:T(8,128)}, f32[256,128]{0,1:T(8,128)}, u32[]{:S(2)}, u32[]{:S(2)}) collective-permute-start(f32[256,128]{0,1:T(8,128)} %get-tuple-element.12), channel_id=1, source_target_pairs={{0,28},{4,0},{8,4},{12,8},{16,12},{20,16},{24,20},{28,24},{1,29},{... | collective-permute-start | bytes 393224 | tf_op jit(solution)/shard_map/ppermute | solution.py:10
  165.4 10.7 %collective-permute-start.8 = (f32[256,128]{0,1:T(8,128)}, f32[256,128]{0,1:T(8,128)}, u32[]{:S(2)}, u32[]{:S(2)}) collective-permute-start(f32[256,128]{0,1:T(8,128)} %get-tuple-element.10), channel_id=1, source_target_pairs={{0,4},{4,8},{8,12},{12,16},{16,20},{20,24},{24,28},{28,0},{1,5},{5... | collective-permute-start | bytes 393224 | tf_op jit(solution)/shard_map/ppermute | solution.py:10
  165.5 14.7 %collective-permute-start.11 = (f32[256,128]{0,1:T(8,128)}, f32[256,128]{0,1:T(8,128)}, u32[]{:S(2)}, u32[]{:S(2)}) collective-permute-start(f32[256,128]{0,1:T(8,128)} %get-tuple-element.11), channel_id=1, source_target_pairs={{0,3},{1,0},{2,1},{3,2},{4,7},{5,4},{6,5},{7,6},{8,11},{9,8},{10,9... | collective-permute-start | bytes 393224 | tf_op jit(solution)/shard_map/ppermute | solution.py:10
  169.2 10.3 %copy-start.7 = (pred[256]{0:T(512)(128)(4,1)S(1)}, pred[256]{0:T(512)(128)(4,1)}, u32[]{:S(2)}) copy-start(pred[256]{0:T(512)(128)(4,1)} %compare_and_fusion.3) | copy-start | bytes 772
  173.8 9.7 %copy-start.5 = (pred[256]{0:T(512)(128)(4,1)S(1)}, pred[256]{0:T(512)(128)(4,1)}, u32[]{:S(2)}) copy-start(pred[256]{0:T(512)(128)(4,1)} %compare_and_fusion) | copy-start | bytes 772
  (1 other events, 1.3 us)
where the time goes:
time: 227 us; the launch traced here: 226 us
  blocking collectives  160 us (70%)
  local copies, waits for them, and re-layouts  28.1 us (12%)
  other arithmetic  15.7 us (7%)
  starting transfers between devices  15.5 us (7%)
  matrix products  4.13 us (2%)
    all_gather x1, blocking collectives, on_device(): values = lax.all_gather(coarse_load, ('sub', 'col'), axis=0, tiled=True)  41.2 us
    psum x1, blocking collectives, inner(): lax.psum(0.5 * jnp.sum(left_field * right_field, axis=0), ('sub', 'col'))  39.9 us
    unnamed x1, blocking collectives  37.7 us
    all_gather x1, blocking collectives, on_device(): piece = lax.all_gather(block_rows, 'sub', axis=0, tiled=True)  30.5 us
    gather x24, local copies, waits for them, and re-layouts, combine(): jnp.take(incoming[number].astype(jnp.float32), places[number], axis=0)  16 us
    ppermute x12, starting transfers between devices, from_behind(): return lax.ppermute(value, axis, pairs)  15.5 us
    psum x1, blocking collectives, on_device(): block_rows = lax.psum(partial_rows, 'col').astype(jnp.bfloat16)  10.3 us
    select_n x14, other arithmetic, combine(): jnp.take(incoming[number].astype(jnp.float32), places[number], axis=0)  8.71 us
  transfers between devices with their start and end apart: 12, of which 1 were waited for; matrix products, arithmetic and copies ran while one was open for 12% of the time, Pallas kernels for 0%

commit v1 on v0

--- a/solution.py
+++ b/solution.py
@@ -42,7 +42,9 @@
         return combine(field, (from_below, from_above, from_left, from_right))
 
     def inner(left_field, right_field):
-        return lax.psum(0.5 * jnp.sum(left_field * right_field, axis=0), ("sub", "col"))
+        return jnp.sum(
+            lax.all_gather(0.5 * jnp.sum(left_field * right_field, axis=0), ("sub", "col")), axis=0
+        )
 
     residual = assemble(rhs[0].astype(jnp.float32))
     weighted = (residual * 0.5).astype(jnp.bfloat16)

time: 227 us -> 265 us (1.17)
  blocking collectives: 160 us -> 198 us
    all_gather x0 -> x2, blocking collectives: none -> 78.5 us  [inner(): lax.all_gather(0.5 * jnp.sum(left_field * right_field, axis=0), ('sub', '...]
    psum x1 -> x0, blocking collectives: 39.9 us -> none  [inner(): lax.psum(0.5 * jnp.sum(left_field * right_field, axis=0), ('sub', 'col'))]
  transfers between devices with their start and end apart: 12 -> 12, of which waited for: 1 -> 1; matrix products, arithmetic and copies ran while one was open for 12% -> 11% of each run, Pallas kernels for 0% -> 0%
where the time goes in v1:
time: 265 us; the launch traced here: 264 us
  blocking collectives  198 us (75%)
  local copies, waits for them, and re-layouts  28.1 us (11%)
  other arithmetic  15.5 us (6%)
  starting transfers between devices  15.5 us (6%)
  matrix products  4.13 us (2%)
    all_gather x2, blocking collectives, inner(): lax.all_gather(0.5 * jnp.sum(left_field * right_field, axis=0), ('sub', '...  78.5 us
    all_gather x1, blocking collectives, on_device(): values = lax.all_gather(coarse_load, ('sub', 'col'), axis=0, tiled=True)  41.2 us
    unnamed x1, blocking collectives  37.7 us
    all_gather x1, blocking collectives, on_device(): piece = lax.all_gather(block_rows, 'sub', axis=0, tiled=True)  30.5 us
    gather x24, local copies, waits for them, and re-layouts, combine(): jnp.take(incoming[number].astype(jnp.float32), places[number], axis=0)  16 us
    ppermute x12, starting transfers between devices, from_behind(): return lax.ppermute(value, axis, pairs)  15.5 us
    psum x1, blocking collectives, on_device(): block_rows = lax.psum(partial_rows, 'col').astype(jnp.bfloat16)  10.3 us
    select_n x14, other arithmetic, combine(): jnp.take(incoming[number].astype(jnp.float32), places[number], axis=0)  8.59 us
  transfers between devices with their start and end apart: 12, of which 1 were waited for; matrix products, arithmetic and copies ran while one was open for 11% of the time, Pallas kernels for 0%

profile of v1, /device:TPU:0, one launch (start us, length us, event | category | flops | bytes accessed | tf_op | source)
XLA Modules:
  0.0 264.3 jit_solution(2077956671415172602)
XLA Ops:
  1.3 3.1 %collective-permute-start = (f32[256,128]{0,1:T(8,128)S(1)}, f32[256,128]{0,1:T(8,128)S(1)}, u32[]{:S(2)}, u32[]{:S(2)}) collective-permute-start(f32[256,128]{0,1:T(8,128)S(1)} %get-tuple-element.14), channel_id=1, source_target_pairs={{0,4},{4,8},{8,12},{12,16},{16,20},{20,24},{24,28},{28,0},{1,5},{5... | collective-permute-start | bytes 393224 | tf_op jit(solution)/shard_map/ppermute | solution.py:10
  4.4 3.1 %collective-permute-start.1 = (f32[256,128]{0,1:T(8,128)S(1)}, f32[256,128]{0,1:T(8,128)S(1)}, u32[]{:S(2)}, u32[]{:S(2)}) collective-permute-start(f32[256,128]{0,1:T(8,128)S(1)} %get-tuple-element.15), channel_id=1, source_target_pairs={{0,28},{4,0},{8,4},{12,8},{16,12},{20,16},{24,20},{28,24},{1,29},{... | collective-permute-start | bytes 393224 | tf_op jit(solution)/shard_map/ppermute | solution.py:10
  12.4 37.7 %all-reduce = s32[256]{0:T(256)S(1)} all-reduce(s32[256]{0:T(256)S(1)} %bitcast_dynamic-update-slice_fusion), channel_id=2, replica_groups=mesh['sub'=8,'col'=4] {'sub','col'}, use_global_device_ids=true, to_apply=%add | all-reduce | flops 256 | bytes 2048
  52.8 1.3 broadcast_select_fusion.9
  57.3 41.2 %all_gather.18 = bf16[256,128]{1,0:T(8,128)(2,1)S(1)} all-gather(bf16[8,128]{1,0:T(8,128)(2,1)S(1)} %fusion.9), channel_id=1, replica_groups=mesh['sub'=8,'col'=4] {'sub','col'}, dimensions={0}, use_global_device_ids=true | all-gather | bytes 67584 | tf_op jit(solution)/shard_map/all_gather | solution.py:56
  98.5 1.3 scatter_custom_fusion
  99.9 10.3 %psum.7 = bf16[32,128]{1,0:T(8,128)(2,1)S(1)} all-reduce(f32[32,128]{1,0:T(8,128)S(1)} %convolution_bitcast_fusion), channel_id=1, replica_groups=mesh['sub'=8,'col'=4] {'col'}, use_global_device_ids=true, to_apply=%region_1.3 | all-reduce | flops 4096 | bytes 24576 | tf_op jit(solution)/shard_map/psum | solution.py:63
  110.3 30.5 %all_gather.19 = bf16[256,128]{1,0:T(8,128)(2,1)S(1)} all-gather(bf16[32,128]{1,0:T(8,128)(2,1)S(1)} %psum.7), channel_id=1, replica_groups=mesh['sub'=8,'col'=4] {'sub'}, dimensions={0}, use_global_device_ids=true | all-gather | bytes 73728 | tf_op jit(solution)/shard_map/all_gather | solution.py:64
  140.8 1.6 fusion.2
  143.1 1.4 fusion.8
  146.6 4.7 %collective-permute-start.5 = (f32[256,128]{0,1:T(8,128)}, f32[256,128]{0,1:T(8,128)S(1)}, u32[]{:S(2)}, u32[]{:S(2)}) collective-permute-start(f32[256,128]{0,1:T(8,128)} %get-tuple-element.13), channel_id=1, source_target_pairs={{0,28},{4,0},{8,4},{12,8},{16,12},{20,16},{24,20},{28,24},{1,29},{... | collective-permute-start | bytes 393224 | tf_op jit(solution)/shard_map/ppermute | solution.py:10
  151.8 1.3 broadcast_select_fusion.8
  153.2 2.2 collective-permute-done.6
  163.3 2.0 collective-permute-start.9
  165.3 1.4 collective-permute-start.11
  167.7 1.3 gather_fusion.11
  170.0 1.3 broadcast_select_fusion.1
  172.3 1.3 gather_fusion.10
  174.7 1.3 broadcast_select_fusion.2
  176.9 1.3 gather_fusion.9
  180.9 1.3 gather_fusion.12
  183.3 1.5 fusion.15
  184.8 41.8 %all-gather.3 = f32[32,1,128]{2,1,0:T(1,128)S(1)} all-gather(f32[1,1,128]{2,1,0:T(1,128)S(1)} %multiply_bitcast_fusion.1), channel_id=3, replica_groups=mesh['sub'=8,'col'=4] {'sub','col'}, dimensions={0}, use_global_device_ids=true | all-gather | bytes 16896 | tf_op jit(solution)/shard_map/all_gather | solution.py:46
  226.6 36.7 %all-gather.4 = f32[32,1,128]{2,1,0:T(1,128)S(1)} all-gather(f32[1,1,128]{2,1,0:T(1,128)S(1)} %multiply_bitcast_fusion), channel_id=4, replica_groups=mesh['sub'=8,'col'=4] {'sub','col'}, dimensions={0}, use_global_device_ids=true | all-gather | bytes 16896 | tf_op jit(solution)/shard_map/all_gather | solution.py:46
  (127 shorter events, 32.8 us)
Async XLA Ops:
  0.0 140.8 %copy-start = (bf16[1,1024,1024]{2,1,0:T(8,128)(2,1)S(1)}, bf16[1,1024,1024]{2,1,0:T(8,128)(2,1)}, u32[]{:S(2)}) copy-start(bf16[1,1024,1024]{2,1,0:T(8,128)(2,1)} %param.11) | copy-start | bytes 6291460
  0.0 9.0 %copy-start.9 = (s32[1,1024]{1,0:T(1,128)S(1)}, s32[1,1024]{1,0:T(1,128)}, u32[]{:S(2)}) copy-start(s32[1,1024]{1,0:T(1,128)} %param.15) | copy-start | bytes 12292
  0.0 11.1 %copy-start.12 = (s32[1,8]{1,0:T(1,128)S(1)}, s32[1,8]{1,0:T(1,128)}, u32[]{:S(2)}) copy-start(s32[1,8]{1,0:T(1,128)} %param.14) | copy-start | bytes 100
  1.3 52.7 %collective-permute-start = (f32[256,128]{0,1:T(8,128)S(1)}, f32[256,128]{0,1:T(8,128)S(1)}, u32[]{:S(2)}, u32[]{:S(2)}) collective-permute-start(f32[256,128]{0,1:T(8,128)S(1)} %get-tuple-element.14), channel_id=1, source_target_pairs={{0,4},{4,8},{8,12},{12,16},{16,20},{20,24},{24,28},{28,0},{1,5},{5... | collective-permute-start | bytes 393224 | tf_op jit(solution)/shard_map/ppermute | solution.py:10
  4.4 50.6 %collective-permute-start.1 = (f32[256,128]{0,1:T(8,128)S(1)}, f32[256,128]{0,1:T(8,128)S(1)}, u32[]{:S(2)}, u32[]{:S(2)}) collective-permute-start(f32[256,128]{0,1:T(8,128)S(1)} %get-tuple-element.15), channel_id=1, source_target_pairs={{0,28},{4,0},{8,4},{12,8},{16,12},{20,16},{24,20},{28,24},{1,29},{... | collective-permute-start | bytes 393224 | tf_op jit(solution)/shard_map/ppermute | solution.py:10
  7.5 48.5 %collective-permute-start.3 = (f32[256,128]{0,1:T(8,128)S(1)}, f32[256,128]{0,1:T(8,128)S(1)}, u32[]{:S(2)}, u32[]{:S(2)}) collective-permute-start(f32[256,128]{0,1:T(8,128)S(1)} %get-tuple-element.16), channel_id=1, source_target_pairs={{0,3},{1,0},{2,1},{3,2},{4,7},{5,4},{6,5},{7,6},{8,11},{9,8},{10,9... | collective-permute-start | bytes 393224 | tf_op jit(solution)/shard_map/ppermute | solution.py:10
  9.0 42.3 %collective-permute-start.2 = (bf16[256,128]{1,0:T(8,128)(2,1)S(1)}, bf16[256,128]{1,0:T(8,128)(2,1)S(1)}, u32[]{:S(2)}, u32[]{:S(2)}) collective-permute-start(bf16[256,128]{1,0:T(8,128)(2,1)S(1)} %slice_bitcast_fusion.3), channel_id=1, source_target_pairs={{0,1},{1,2},{2,3},{3,0},{4,5},{5,6},{6,7},{7,4},{8,9},{9,10},{10,1... | collective-permute-start | bytes 196616 | tf_op jit(solution)/shard_map/ppermute | solution.py:10
  54.9 2.0 copy-start.6
  54.9 2.1 copy-start.8
  54.9 2.1 copy-start.4
  55.9 43.9 %copy-start.3 = (bf16[32,64]{1,0:T(8,128)(2,1)S(1)}, bf16[32,64]{1,0:T(8,128)(2,1)}, u32[]{:S(2)}) copy-start(bf16[32,64]{1,0:T(8,128)(2,1)} %param.13) | copy-start | bytes 12292
  57.0 86.1 %copy-start.10 = (pred[8]{0:T(512)(128)(4,1)S(1)}, pred[8]{0:T(512)(128)(4,1)}, u32[]{:S(2)}) copy-start(pred[8]{0:T(512)(128)(4,1)} %and_bitcast_fusion) | copy-start | bytes 28
  57.0 86.1 %copy-start.11 = (pred[8]{0:T(512)(128)(4,1)S(1)}, pred[8]{0:T(512)(128)(4,1)}, u32[]{:S(2)}) copy-start(pred[8]{0:T(512)(128)(4,1)} %compare_and_fusion.4) | copy-start | bytes 28
  146.6 9.7 %collective-permute-start.4 = (f32[256,128]{0,1:T(8,128)}, f32[256,128]{0,1:T(8,128)S(1)}, u32[]{:S(2)}, u32[]{:S(2)}) collective-permute-start(f32[256,128]{0,1:T(8,128)} %get-tuple-element.11), channel_id=1, source_target_pairs={{0,4},{4,8},{8,12},{12,16},{16,20},{20,24},{24,28},{28,0},{1,5},{5... | collective-permute-start | bytes 393224 | tf_op jit(solution)/shard_map/ppermute | solution.py:10
  146.6 10.6 %collective-permute-start.5 = (f32[256,128]{0,1:T(8,128)}, f32[256,128]{0,1:T(8,128)S(1)}, u32[]{:S(2)}, u32[]{:S(2)}) collective-permute-start(f32[256,128]{0,1:T(8,128)} %get-tuple-element.13), channel_id=1, source_target_pairs={{0,28},{4,0},{8,4},{12,8},{16,12},{20,16},{24,20},{28,24},{1,29},{... | collective-permute-start | bytes 393224 | tf_op jit(solution)/shard_map/ppermute | solution.py:10
  151.3 6.8 %collective-permute-start.7 = (f32[256,128]{0,1:T(8,128)}, f32[256,128]{0,1:T(8,128)}, u32[]{:S(2)}, u32[]{:S(2)}) collective-permute-start(f32[256,128]{0,1:T(8,128)} %get-tuple-element.12), channel_id=1, source_target_pairs={{0,3},{1,0},{2,1},{3,2},{4,7},{5,4},{6,5},{7,6},{8,11},{9,8},{10,9... | collective-permute-start | bytes 393224 | tf_op jit(solution)/shard_map/ppermute | solution.py:10
  151.3 4.0 %collective-permute-start.6 = (bf16[256,128]{0,1:T(8,128)(2,1)S(1)}, bf16[256,128]{0,1:T(8,128)(2,1)S(1)}, u32[]{:S(2)}, u32[]{:S(2)}) collective-permute-start(bf16[256,128]{0,1:T(8,128)(2,1)S(1)} %slice.134), channel_id=1, source_target_pairs={{0,1},{1,2},{2,3},{3,0},{4,5},{5,6},{6,7},{7,4},{8,9},{9,10},{10,1... | collective-permute-start | bytes 196616 | tf_op jit(solution)/shard_map/ppermute | solution.py:10
  160.0 1.6 copy-start.1
  162.5 4.2 %collective-permute-start.10 = (bf16[256,128]{0,1:T(8,128)(2,1)S(1)}, bf16[256,128]{0,1:T(8,128)(2,1)}, u32[]{:S(2)}, u32[]{:S(2)}) collective-permute-start(bf16[256,128]{0,1:T(8,128)(2,1)S(1)} %slice.133), channel_id=1, source_target_pairs={{0,1},{1,2},{2,3},{3,0},{4,5},{5,6},{6,7},{7,4},{8,9},{9,10},{10,1... | collective-permute-start | bytes 196616 | tf_op jit(solution)/shard_map/ppermute | solution.py:10
  163.3 8.0 %collective-permute-start.9 = (f32[256,128]{0,1:T(8,128)}, f32[256,128]{0,1:T(8,128)}, u32[]{:S(2)}, u32[]{:S(2)}) collective-permute-start(f32[256,128]{0,1:T(8,128)} %get-tuple-element.10), channel_id=1, source_target_pairs={{0,28},{4,0},{8,4},{12,8},{16,12},{20,16},{24,20},{28,24},{1,29},{... | collective-permute-start | bytes 393224 | tf_op jit(solution)/shard_map/ppermute | solution.py:10
  165.3 10.7 %collective-permute-start.8 = (f32[256,128]{0,1:T(8,128)}, f32[256,128]{0,1:T(8,128)}, u32[]{:S(2)}, u32[]{:S(2)}) collective-permute-start(f32[256,128]{0,1:T(8,128)} %get-tuple-element.8), channel_id=1, source_target_pairs={{0,4},{4,8},{8,12},{12,16},{16,20},{20,24},{24,28},{28,0},{1,5},{5... | collective-permute-start | bytes 393224 | tf_op jit(solution)/shard_map/ppermute | solution.py:10
  165.3 14.6 %collective-permute-start.11 = (f32[256,128]{0,1:T(8,128)}, f32[256,128]{0,1:T(8,128)}, u32[]{:S(2)}, u32[]{:S(2)}) collective-permute-start(f32[256,128]{0,1:T(8,128)} %get-tuple-element.9), channel_id=1, source_target_pairs={{0,3},{1,0},{2,1},{3,2},{4,7},{5,4},{6,5},{7,6},{8,11},{9,8},{10,9... | collective-permute-start | bytes 393224 | tf_op jit(solution)/shard_map/ppermute | solution.py:10
  169.0 10.3 %copy-start.7 = (pred[256]{0:T(512)(128)(4,1)S(1)}, pred[256]{0:T(512)(128)(4,1)}, u32[]{:S(2)}) copy-start(pred[256]{0:T(512)(128)(4,1)} %compare_and_fusion.3) | copy-start | bytes 772
  173.6 9.6 %copy-start.5 = (pred[256]{0:T(512)(128)(4,1)S(1)}, pred[256]{0:T(512)(128)(4,1)}, u32[]{:S(2)}) copy-start(pred[256]{0:T(512)(128)(4,1)} %compare_and_fusion) | copy-start | bytes 772
  (1 other events, 1.3 us)
